TPU v7x, 128 devices: a whole 4x4x4 slice. The times are simulated.
128 devices in a mesh: bx: 4 (over y), by: 4 (over x), bz: 8 (over z, core).
Axes of the slice: x: 4, y: 4, z: 4, core: 2. Of those that a mesh axis runs over, the one named last changes fastest.
Arguments:
- position: float32 [3, 128, 128, 2048], P(None, 'bx', 'by', 'bz'), may hold values from -2 to 2
- velocity: float32 [3, 128, 128, 2048], P(None, 'bx', 'by', 'bz'), may hold values from -3 to 3
- density: float32 [128, 128, 2048], P('bx', 'by', 'bz'), may hold values from 0.5 to 2
- energy: float32 [128, 128, 2048], P('bx', 'by', 'bz'), may hold values from 0.1 to 10
- pinned: int32 [128, 128, 2048], P('bx', 'by', 'bz'), may hold values 0 or 1
Outputs:
- velocity_new: float32 [3, 128, 128, 2048], P(None, 'bx', 'by', 'bz')
- accel: float32 [3, 128, 128, 2048], P(None, 'bx', 'by', 'bz')
- relaxed: float32 [3, 128, 128, 2048], P(None, 'bx', 'by', 'bz')
- density_new: float32 [128, 128, 2048], P('bx', 'by', 'bz')
- energy_new: float32 [128, 128, 2048], P('bx', 'by', 'bz')
All inputs are finite; a program needn't handle non-finite values. No bound on the sum of `pinned` on one device may be relied on, other than what follows from the above.
Results may differ from a plain program's by a relative error of at most 0.0003.
Values sent between devices are 32-bit elements; how exact they have to be, the bound alone decides.
A program may use at most 128 MiB of HBM per device.

v0:
```python
import jax
import jax.numpy as jnp
from jax import lax
from jax.sharding import PartitionSpec as P

CG_ITERS = 2
SWEEPS = 3
TIME_STEP = 0.6
RELAX_RATE = 0.8
CONSISTENT = 0.2


def from_behind(x, axis, by):
    length = lax.axis_size(axis)
    pairs = [(i, i + by) for i in range(length) if 0 <= i + by < length]
    return lax.ppermute(x, axis, pairs)


def padded(block, sides, width):
    for axis, dim in sides:
        count = lax.axis_size(axis)
        forward = [(i, i + 1) for i in range(count - 1)]
        backward = [(target, source) for source, target in forward]
        low = lax.ppermute(
            lax.slice_in_dim(block, block.shape[dim] - width, None, axis=dim), axis, forward
        )
        high = lax.ppermute(lax.slice_in_dim(block, 0, width, axis=dim), axis, backward)
        block = jnp.concatenate([low, block, high], axis=dim)
    return block


def shift_triple(along_dim, along, first, second):
    offsets = [0, 0, 0]
    offsets[along_dim] = along
    others = [d for d in range(3) if d != along_dim]
    offsets[others[0]] = first
    offsets[others[1]] = second
    return offsets


def select_at(extended, offsets):
    sizes = extended.shape[-3:]
    return extended[
        ...,
        1 + offsets[0] : sizes[0] - 1 + offsets[0],
        1 + offsets[1] : sizes[1] - 1 + offsets[1],
        1 + offsets[2] : sizes[2] - 1 + offsets[2],
    ]


def corner_force(pressure_ext):
    parts = []
    for along_dim in range(3):
        summed = 0.0
        for first in (0, -1):
            for second in (0, -1):
                summed = (
                    summed
                    + select_at(pressure_ext, shift_triple(along_dim, -1, first, second))
                    - select_at(pressure_ext, shift_triple(along_dim, 0, first, second))
                )
        parts.append(0.25 * summed)
    return jnp.stack(parts)


def node_mass(density_ext):
    summed = 0.0
    for first in (0, -1):
        for second in (0, -1):
            for third in (0, -1):
                summed = summed + select_at(density_ext, [first, second, third])
    return 0.125 * summed


def neighbours(extended):
    summed = 0.0
    for along_dim in range(3):
        for along in (-1, 1):
            summed = summed + select_at(extended, shift_triple(along_dim, along, 0, 0))
    return summed


def divergence(vel_ext):
    summed = 0.0
    for along_dim in range(3):
        for first in (0, 1):
            for second in (0, 1):
                summed = (
                    summed
                    + select_at(vel_ext[along_dim], shift_triple(along_dim, 1, first, second))
                    - select_at(vel_ext[along_dim], shift_triple(along_dim, 0, first, second))
                )
    return 0.25 * summed


def face_flux(packed, along_dim, along):
    speed = 0.0
    for first in (0, 1):
        for second in (0, 1):
            speed = speed + select_at(
                packed[along_dim], shift_triple(along_dim, along, first, second)
            )
    speed = 0.25 * speed
    upper = select_at(packed[3:5], shift_triple(along_dim, along, 0, 0))
    lower = select_at(packed[3:5], shift_triple(along_dim, along - 1, 0, 0))
    return speed * jnp.where(speed > 0, upper, lower)


def remap_cells(packed):
    result = select_at(packed[3:5], [0, 0, 0])
    for along_dim in range(3):
        result = result + face_flux(packed, along_dim, 1) - face_flux(packed, along_dim, 0)
    return result


def inner(first, second):
    return jnp.sum(first * second, axis=(1, 2, 3), keepdims=True)


def lower_cells(values):
    got = from_behind(values[..., -1:, :, :], "bx", 1)
    widened = jnp.concatenate([got, values], axis=-3)
    got = from_behind(widened[..., :, -1:, :], "by", 1)
    widened = jnp.concatenate([got, widened], axis=-2)
    got = from_behind(widened[..., :, :, -1:], "bz", 1)
    widened = jnp.concatenate([got, widened], axis=-1)
    return jnp.pad(widened, [(0, 0)] * (values.ndim - 3) + [(0, 1)] * 3)


def upper_nodes(values):
    got = from_behind(values[..., :1, :, :], "bx", -1)
    widened = jnp.concatenate([values, got], axis=-3)
    got = from_behind(widened[..., :, :1, :], "by", -1)
    widened = jnp.concatenate([widened, got], axis=-2)
    got = from_behind(widened[..., :, :, :1], "bz", -1)
    widened = jnp.concatenate([widened, got], axis=-1)
    return jnp.pad(widened, [(0, 0)] * (values.ndim - 3) + [(1, 0)] * 3)


def mass_apply(vector, masses):
    extended = padded(vector, (("bx", 1), ("by", 2), ("bz", 3)), 1)
    return masses * vector + CONSISTENT * (6.0 * vector + neighbours(extended))


def squares(residual):
    return lax.psum(inner(residual, residual), ("bx", "by", "bz"))


def one_sweep(relaxed, free):
    extended = padded(relaxed, (("bx", 1), ("by", 2), ("bz", 3)), 1)
    return relaxed + RELAX_RATE * free * (neighbours(extended) / 6.0 - relaxed)


def on_device(position, velocity, density, energy, pinned):
    cells = lower_cells(jnp.stack([density, energy]))
    force = corner_force(0.4 * cells[0] * cells[1])
    masses = node_mass(cells[0])
    solution = jnp.zeros_like(force)
    residual = force
    direction = force
    norm_now = squares(residual)
    for step_index in range(CG_ITERS):
        image = mass_apply(direction, masses)
        alpha = norm_now / lax.psum(inner(direction, image), ("bx", "by", "bz"))
        solution = solution + alpha * direction
        residual = residual - alpha * image
        norm_next = squares(residual)
        direction = residual + norm_next / norm_now * direction
        norm_now = norm_next
    velocity_new = velocity + TIME_STEP * solution
    vel_ext = upper_nodes(velocity_new)
    spread = divergence(vel_ext)
    pressure = 0.4 * density * energy
    energy_lag = energy - TIME_STEP * pressure * spread / density
    moved = position + TIME_STEP * velocity_new
    free = 1.0 - pinned.astype(jnp.float32)
    relaxed = moved
    for step_index in range(SWEEPS):
        relaxed = one_sweep(relaxed, free)
    packed = padded(
        jnp.concatenate([relaxed - moved, density[None], (density * energy_lag)[None]]),
        (("bx", 1), ("by", 2), ("bz", 3)),
        1,
    )
    remapped = remap_cells(packed)
    return (velocity_new, solution, relaxed, remapped[0], remapped[1])


def solution(mesh):
    in_specs = (
        P(None, "bx", "by", "bz"),
        P(None, "bx", "by", "bz"),
        P("bx", "by", "bz"),
        P("bx", "by", "bz"),
        P("bx", "by", "bz"),
    )
    out_specs = (
        P(None, "bx", "by", "bz"),
        P(None, "bx", "by", "bz"),
        P(None, "bx", "by", "bz"),
        P("bx", "by", "bz"),
        P("bx", "by", "bz"),
    )
    return jax.shard_map(
        on_device, mesh=mesh, in_specs=in_specs, out_specs=out_specs, check_vma=False
    )
```

profile of v0, /device:TPU:1, one launch (start us, length us, event | category | flops | bytes accessed | tf_op | source)
XLA Modules:
  0.0 638.1 jit_solution(13406718772434215634)
XLA Ops:
  1.6 4.0 collective-permute-start
  14.1 5.8 collective-permute-start.2
  29.0 4.0 collective-permute-start.3
  38.5 4.0 collective-permute-start.5
  45.3 4.1 collective-permute-done.6
  61.2 5.9 collective-permute-start.7
  67.1 7.7 %fusion.120 = f32[32,32,256]{2,1,0:T(8,128)} fusion(f32[34,34,258]{2,1,0:T(8,128)} %slice_bitcast_fusion.7), kind=kLoop, calls=%fused_computation.316 | loop fusion | flops 2097152 | bytes 9437184 | tf_op jit(solution)/shard_map/mul | solution.py:72
  80.7 16.0 %multiply_reduce_fusion.1 = (f32[3]{0:T(128)}, f32[3]{0:T(128)}, f32[3,32,32,256]{3,2,1,0:T(8,128)}) fusion(f32[1,32,32,256]{3,2,1,0:T(8,128)} %copy-done.4, f32[1,32,32,256]{3,2,1,0:T(8,128)S(1)} %multiply_bitcast_fusion.1, f32[1,32,32,256]{3,2,1,0:T(8,128)S(1)} %get-tuple-element.82, f32[3,34,34,1]{3,2,1,0:T(8,128)} %copy.67, ...), kind=kLoop, calls=%fused_computation.195 | loop fusion | flops 36175864 | bytes 7773304 | tf_op jit(solution)/shard_map/reduce_sum | solution.py:117
  96.7 64.6 %all-reduce.2 = (f32[3,1,1,1]{0,3,2,1:T(1,128)S(1)}, f32[3,1,1,1]{0,3,2,1:T(1,128)S(1)}) all-reduce(f32[3,1,1,1]{0,3,2,1:T(1,128)} %bitcast.58, f32[3,1,1,1]{0,3,2,1:T(1,128)} %bitcast.57), channel_id=1, replica_groups=mesh['bx'=4,'by'=4,'bz'=8] {'bx','by','bz'}, use_global_device_ids=true, to_apply=%region_1.2 | all-reduce | flops 6 | bytes 48 | tf_op jit(solution)/shard_map/psum | solution.py:146
  164.2 63.1 %psum.30 = f32[3,1,1,1]{0,3,2,1:T(1,128)S(1)} all-reduce(f32[3,1,1,1]{0,3,2,1:T(1,128)S(1)} %bitcast.60), channel_id=1, replica_groups=mesh['bx'=4,'by'=4,'bz'=8] {'bx','by','bz'}, use_global_device_ids=true, to_apply=%region_5.6 | all-reduce | flops 3 | bytes 24 | tf_op jit(solution)/shard_map/psum | solution.py:146
  251.8 5.8 collective-permute-start.13
  269.3 15.8 %fusion.67 = f32[3]{0:T(128)} fusion(f32[3,32,32,256]{3,2,1,0:T(8,128)} %copy-done.5, f32[3,34,34,1]{3,2,1,0:T(8,128)} %copy.71, f32[3,34,1,256]{3,2,1,0:T(1,128)S(1)} %collective-permute-done.12, f32[3,34,1,256]{3,2,1,0:T(1,128)S(1)} %collective-permute-done.11, f32[3,1,32,256]{3,2,1,0:T(8,128)S(1)} %collective-permute-done.10, ...), kind=kLoop, calls=%fused_computation.147 | loop fusion | flops 23592956 | bytes 4627564 | tf_op jit(solution)/shard_map/reduce_sum | solution.py:117
  285.1 63.9 %psum.31 = f32[3,1,1,1]{0,3,2,1:T(1,128)S(1)} all-reduce(f32[3,1,1,1]{0,3,2,1:T(1,128)} %bitcast.59), channel_id=1, replica_groups=mesh['bx'=4,'by'=4,'bz'=8] {'bx','by','bz'}, use_global_device_ids=true, to_apply=%region_7.8 | all-reduce | flops 3 | bytes 24 | tf_op jit(solution)/shard_map/psum | solution.py:164
  349.7 6.8 %multiply_add_fusion = (f32[3,32,32,256]{3,2,1,0:T(8,128)S(1)}, f32[3,32,32,256]{3,2,1,0:T(8,128)}, f32[3,32,32,256]{3,2,1,0:T(8,128)}) fusion(f32[3,32,32,256]{3,2,1,0:T(8,128)} %param.5, f32[3,32,32,256]{3,2,1,0:T(8,128)} %param.6, f32[3]{0:T(128)S(1)} %divide_bitcast_fusion, f32[1,32,32,256]{3,2,1,0:T(8,128)} %copy-done.4, ...), kind=kLoop, calls=%fused_computation.189 | loop fusion | flops 10223616 | bytes 22020132 | tf_op jit(solution)/shard_map/add | solution.py:175
  365.6 4.0 collective-permute-start.17
  378.9 5.4 collective-permute-start.20
  392.2 14.2 %fusion.57 = f32[3,32,32,256]{3,2,1,0:T(8,128)S(1)} fusion(f32[3,32,32,256]{3,2,1,0:T(8,128)} %copy-done.3, f32[3,34,34,1]{3,2,1,0:T(8,128)} %copy.81, f32[3,34,1,256]{3,2,1,0:T(1,128)S(1)} %copy.75, f32[3,34,1,256]{3,2,1,0:T(1,128)S(1)} %copy.73, f32[3,1,32,256]{3,2,1,0:T(8,128)S(1)} %collective-permute-done.16, ...), kind=kLoop, calls=%fused_computation.119 | loop fusion | flops 21233664 | bytes 7773280 | tf_op jit(solution)/shard_map/add | solution.py:151
  416.1 4.7 collective-permute-start.23
  422.2 4.3 collective-permute-done.34
  435.3 5.6 collective-permute-start.26
  462.1 14.5 %fusion.48 = f32[3,32,32,256]{3,2,1,0:T(8,128)S(1)} fusion(f32[3,32,32,256]{3,2,1,0:T(8,128)} %copy-done.6, f32[3,34,34,1]{3,2,1,0:T(8,128)} %copy.91, f32[3,34,1,256]{3,2,1,0:T(1,128)S(1)} %copy.85, f32[3,34,1,256]{3,2,1,0:T(1,128)S(1)} %copy.83, f32[3,1,32,256]{3,2,1,0:T(8,128)S(1)} %collective-permute-done.22, ...), kind=kLoop, calls=%fused_computation.92 | loop fusion | flops 21233664 | bytes 7773280 | tf_op jit(solution)/shard_map/add | solution.py:151
  481.2 4.7 select_maximum_fusion
  487.4 4.7 collective-permute-start.29
  510.0 20.4 %fusion.119 = f32[1,32,32,256]{3,2,1,0:T(8,128)} fusion(f32[32,32,256]{2,1,0:T(8,128)S(1)} %copy-done, f32[32,32,256]{2,1,0:T(8,128)} %param.8, f32[34,34,258]{2,1,0:T(8,128)} %get-tuple-element.39, f32[34,34,258]{2,1,0:T(8,128)} %get-tuple-element.38, f32[34,34,258]{2,1,0:T(8,128)S(1)} %get-tuple-element.37), kind=kLoop, calls=%fused_computation.292 | loop fusion | flops 8126464 | bytes 28311552 | tf_op jit(solution)/shard_map/broadcast_in_dim | solution.py:181
  536.4 16.5 %fusion.127 = (f32[3,32,32,256]{3,2,1,0:T(8,128)S(1)}, f32[3,32,32,256]{3,2,1,0:T(8,128)}) fusion(f32[3,32,32,256]{3,2,1,0:T(8,128)} %copy-done.3, f32[3,32,32,256]{3,2,1,0:T(8,128)} %copy-done.7, f32[3,34,34,1]{3,2,1,0:T(8,128)} %copy.101, f32[3,34,1,256]{3,2,1,0:T(1,128)S(1)} %copy.95, f32[3,1,32,256]{3,2,1,0:T(8,128)S(1)} %collective-permute-done.28, ...), kind=kLoop, calls=%fused_computation.365 | loop fusion | flops 22020096 | bytes 14064736 | tf_op jit(solution)/shard_map/sub | solution.py:181
  552.9 4.0 collective-permute-start.36
  560.8 4.1 collective-permute-done.37
  571.8 3.8 collective-permute-done.39
  577.2 3.9 fusion.130
  600.7 16.1 %pad_maximum_fusion = f32[5,34,34,258]{3,2,1,0:T(8,128)S(1)} fusion(f32[5,34,34,1]{3,2,1,0:T(8,128)} %copy.109, f32[5,34,1,256]{3,2,1,0:T(1,128)} %copy-done.19, f32[5,1,32,256]{3,2,1,0:T(8,128)S(1)} %collective-permute-done.37, f32[1,32,32,256]{3,2,1,0:T(8,128)} %fusion.119, f32[1,32,32,256]{3,2,1,0:T(8,128)} %bitcast.46, ...), kind=kLoop, calls=%fused_computation | loop fusion | flops 11929920 | bytes 11929920 | tf_op jit(solution)/shard_map/concatenate | solution.py:28
  621.0 6.0 broadcast_compare_fusion.1
  627.1 9.3 %fusion.84 = f32[2,32,32,256]{3,2,1,0:T(8,128)S(1)} fusion(f32[3,32,32,256]{3,2,1,0:T(8,128)S(1)} %get-tuple-element.26, f32[1,32,32,256]{3,2,1,0:T(8,128)S(1)} %bitcast.52, f32[5,34,34,1]{3,2,1,0:T(8,128)S(1)} %copy-done.13, f32[5,34,1,256]{3,2,1,0:T(1,128)S(1)} %copy-done.20, f32[5,34,1,256]{3,2,1,0:T(1,128)S(1)} %copy-done.18, ...), kind=kLoop, calls=%fused_computation.206 | loop fusion | flops 25690112 | bytes 15926432 | tf_op jit(solution)/shard_map/sub | solution.py:112
  (205 shorter events, 218.7 us)
Async XLA Ops:
  14.1 6.8 %collective-permute-start.2 = (f32[2,33,33,1]{2,0,3,1:T(2,128)S(1)}, f32[2,33,33,1]{2,0,3,1:T(2,128)}, u32[]{:S(2)}, u32[]{:S(2)}) collective-permute-start(f32[2,33,33,1]{2,0,3,1:T(2,128)S(1)} %copy.62), channel_id=1, source_target_pairs={{0,1},{1,2},{2,3},{3,4},{4,5},{5,6},{6,7},{8,9},{9,10},{10,11},{11... | collective-permute-start | bytes 26144 | tf_op jit(solution)/shard_map/ppermute | solution.py:16
  29.0 5.6 collective-permute-start.3
  38.5 6.8 %collective-permute-start.5 = (f32[3,34,1,256]{3,2,1,0:T(1,128)S(1)}, f32[3,34,1,256]{3,2,1,0:T(1,128)S(1)}, u32[]{:S(2)}, u32[]{:S(2)}) collective-permute-start(f32[3,34,1,256]{3,2,1,0:T(1,128)S(1)} %get-tuple-element.62), channel_id=1, source_target_pairs={{0,8},{8,16},{16,24},{1,9},{9,17},{17,25},{2,10},{10,18},{18,26},{... | collective-permute-start | bytes 313352 | tf_op jit(solution)/shard_map/ppermute | solution.py:24
  42.5 6.8 %collective-permute-start.6 = (f32[3,34,1,256]{3,2,1,0:T(1,128)S(1)}, f32[3,34,1,256]{3,2,1,0:T(1,128)S(1)}, u32[]{:S(2)}, u32[]{:S(2)}) collective-permute-start(f32[3,34,1,256]{3,2,1,0:T(1,128)S(1)} %get-tuple-element.63), channel_id=1, source_target_pairs={{8,0},{16,8},{24,16},{9,1},{17,9},{25,17},{10,2},{18,10},{26,18},{... | collective-permute-start | bytes 313352 | tf_op jit(solution)/shard_map/ppermute | solution.py:27
  58.9 18.8 %collective-permute-start.8 = (f32[3,34,34,1]{2,3,1,0:T(1,128)}, f32[3,34,34,1]{2,3,1,0:T(1,128)}, u32[]{:S(2)}, u32[]{:S(2)}) collective-permute-start(f32[3,34,34,1]{2,3,1,0:T(1,128)} %copy.66), channel_id=1, source_target_pairs={{1,0},{2,1},{3,2},{4,3},{5,4},{6,5},{7,6},{9,8},{10,9},{11,10},{12... | collective-permute-start | bytes 41624 | tf_op jit(solution)/shard_map/ppermute | solution.py:27
  61.2 13.6 %collective-permute-start.7 = (f32[3,34,34,1]{2,3,1,0:T(1,128)}, f32[3,34,34,1]{2,3,1,0:T(1,128)}, u32[]{:S(2)}, u32[]{:S(2)}) collective-permute-start(f32[3,34,34,1]{2,3,1,0:T(1,128)} %copy.64), channel_id=1, source_target_pairs={{0,1},{1,2},{2,3},{3,4},{4,5},{5,6},{6,7},{8,9},{9,10},{10,11},{11... | collective-permute-start | bytes 41624 | tf_op jit(solution)/shard_map/ppermute | solution.py:24
  240.0 5.4 collective-permute-start.12
  251.8 10.9 %collective-permute-start.13 = (f32[3,34,34,1]{2,3,1,0:T(1,128)}, f32[3,34,34,1]{2,3,1,0:T(1,128)}, u32[]{:S(2)}, u32[]{:S(2)}) collective-permute-start(f32[3,34,34,1]{2,3,1,0:T(1,128)} %copy.68), channel_id=1, source_target_pairs={{0,1},{1,2},{2,3},{3,4},{4,5},{5,6},{6,7},{8,9},{9,10},{10,11},{11... | collective-permute-start | bytes 41624 | tf_op jit(solution)/shard_map/ppermute | solution.py:24
  260.6 5.7 collective-permute-start.14
  364.2 5.6 collective-permute-start.18
  365.6 5.8 collective-permute-start.17
  378.9 11.1 %collective-permute-start.20 = (f32[3,34,34,1]{2,1,3,0:T(8,128)}, f32[3,34,34,1]{2,1,3,0:T(8,128)S(1)}, u32[]{:S(2)}, u32[]{:S(2)}) collective-permute-start(f32[3,34,34,1]{2,1,3,0:T(8,128)} %copy.80), channel_id=1, source_target_pairs={{1,0},{2,1},{3,2},{4,3},{5,4},{6,5},{7,6},{9,8},{10,9},{11,10},{12... | collective-permute-start | bytes 41624 | tf_op jit(solution)/shard_map/ppermute | solution.py:27
  406.4 5.5 collective-permute-start.21
  410.6 10.2 %collective-permute-start.33 = (f32[3,1,32,256]{3,2,1,0:T(8,128)S(1)}, f32[3,1,32,256]{3,2,1,0:T(8,128)S(1)}, u32[]{:S(2)}, u32[]{:S(2)}) collective-permute-start(f32[3,1,32,256]{3,2,1,0:T(8,128)S(1)} %slice.782), channel_id=1, source_target_pairs={{32,0},{64,32},{96,64},{33,1},{65,33},{97,65},{34,2},{66,34},{98,6... | collective-permute-start | bytes 294920 | tf_op jit(solution)/shard_map/ppermute | solution.py:16
  414.8 11.8 %collective-permute-start.24 = (f32[3,34,1,256]{3,1,2,0:T(8,128)S(1)}, f32[3,34,1,256]{3,1,2,0:T(8,128)S(1)}, u32[]{:S(2)}, u32[]{:S(2)}) collective-permute-start(f32[3,34,1,256]{3,1,2,0:T(8,128)S(1)} %copy.84), channel_id=1, source_target_pairs={{8,0},{16,8},{24,16},{9,1},{17,9},{25,17},{10,2},{18,10},{26,18},{... | collective-permute-start | bytes 313352 | tf_op jit(solution)/shard_map/ppermute | solution.py:27
  416.1 10.7 %collective-permute-start.23 = (f32[3,34,1,256]{3,1,2,0:T(8,128)S(1)}, f32[3,34,1,256]{3,1,2,0:T(8,128)S(1)}, u32[]{:S(2)}, u32[]{:S(2)}) collective-permute-start(f32[3,34,1,256]{3,1,2,0:T(8,128)S(1)} %copy.82), channel_id=1, source_target_pairs={{0,8},{8,16},{16,24},{1,9},{9,17},{17,25},{2,10},{10,18},{18,26},{... | collective-permute-start | bytes 313352 | tf_op jit(solution)/shard_map/ppermute | solution.py:24
  420.9 5.6 collective-permute-start.34
  435.3 24.7 %collective-permute-start.26 = (f32[3,34,34,1]{2,1,3,0:T(8,128)S(1)}, f32[3,34,34,1]{2,1,3,0:T(8,128)S(1)}, u32[]{:S(2)}, u32[]{:S(2)}) collective-permute-start(f32[3,34,34,1]{2,1,3,0:T(8,128)S(1)} %copy.90), channel_id=1, source_target_pairs={{1,0},{2,1},{3,2},{4,3},{5,4},{6,5},{7,6},{9,8},{10,9},{11,10},{12... | collective-permute-start | bytes 41624 | tf_op jit(solution)/shard_map/ppermute | solution.py:27
  440.9 16.8 %collective-permute-start.25 = (f32[3,34,34,1]{2,1,3,0:T(8,128)S(1)}, f32[3,34,34,1]{2,1,3,0:T(8,128)S(1)}, u32[]{:S(2)}, u32[]{:S(2)}) collective-permute-start(f32[3,34,34,1]{2,1,3,0:T(8,128)S(1)} %copy.88), channel_id=1, source_target_pairs={{0,1},{1,2},{2,3},{3,4},{4,5},{5,6},{6,7},{8,9},{9,10},{10,11},{11... | collective-permute-start | bytes 41624 | tf_op jit(solution)/shard_map/ppermute | solution.py:24
  450.0 5.5 collective-permute-start.35
  476.6 9.3 %collective-permute-start.27 = (f32[3,1,32,256]{3,2,1,0:T(8,128)S(1)}, f32[3,1,32,256]{3,2,1,0:T(8,128)S(1)}, u32[]{:S(2)}, u32[]{:S(2)}) collective-permute-start(f32[3,1,32,256]{3,2,1,0:T(8,128)S(1)} %get-tuple-element.64), channel_id=1, source_target_pairs={{0,32},{32,64},{64,96},{1,33},{33,65},{65,97},{2,34},{34,66},{66,9... | collective-permute-start | bytes 294920 | tf_op jit(solution)/shard_map/ppermute | solution.py:24
  479.9 6.0 collective-permute-start.28
  486.1 8.4 %collective-permute-start.30 = (f32[3,34,1,256]{3,1,2,0:T(8,128)S(1)}, f32[3,34,1,256]{3,1,2,0:T(8,128)S(1)}, u32[]{:S(2)}, u32[]{:S(2)}) collective-permute-start(f32[3,34,1,256]{3,1,2,0:T(8,128)S(1)} %copy.94), channel_id=1, source_target_pairs={{8,0},{16,8},{24,16},{9,1},{17,9},{25,17},{10,2},{18,10},{26,18},{... | collective-permute-start | bytes 313352 | tf_op jit(solution)/shard_map/ppermute | solution.py:27
  487.4 7.2 %collective-permute-start.29 = (f32[3,34,1,256]{3,1,2,0:T(8,128)S(1)}, f32[3,34,1,256]{3,1,2,0:T(8,128)S(1)}, u32[]{:S(2)}, u32[]{:S(2)}) collective-permute-start(f32[3,34,1,256]{3,1,2,0:T(8,128)S(1)} %copy.92), channel_id=1, source_target_pairs={{0,8},{8,16},{16,24},{1,9},{9,17},{17,25},{2,10},{10,18},{18,26},{... | collective-permute-start | bytes 313352 | tf_op jit(solution)/shard_map/ppermute | solution.py:24
  504.5 29.0 %collective-permute-start.32 = (f32[3,34,34,1]{2,1,3,0:T(8,128)}, f32[3,34,34,1]{2,1,3,0:T(8,128)}, u32[]{:S(2)}, u32[]{:S(2)}) collective-permute-start(f32[3,34,34,1]{2,1,3,0:T(8,128)} %copy.100), channel_id=1, source_target_pairs={{1,0},{2,1},{3,2},{4,3},{5,4},{6,5},{7,6},{9,8},{10,9},{11,10},{12... | collective-permute-start | bytes 41624 | tf_op jit(solution)/shard_map/ppermute | solution.py:27
  506.4 24.0 %collective-permute-start.31 = (f32[3,34,34,1]{2,1,3,0:T(8,128)}, f32[3,34,34,1]{2,1,3,0:T(8,128)}, u32[]{:S(2)}, u32[]{:S(2)}) collective-permute-start(f32[3,34,34,1]{2,1,3,0:T(8,128)} %copy.98), channel_id=1, source_target_pairs={{0,1},{1,2},{2,3},{3,4},{4,5},{5,6},{6,7},{8,9},{9,10},{10,11},{11... | collective-permute-start | bytes 41624 | tf_op jit(solution)/shard_map/ppermute | solution.py:24
  552.9 7.9 %collective-permute-start.36 = (f32[5,1,32,256]{3,2,1,0:T(8,128)S(1)}, f32[5,1,32,256]{3,2,1,0:T(8,128)S(1)}, u32[]{:S(2)}, u32[]{:S(2)}) collective-permute-start(f32[5,1,32,256]{3,2,1,0:T(8,128)S(1)} %get-tuple-element.42), channel_id=1, source_target_pairs={{0,32},{32,64},{64,96},{1,33},{33,65},{65,97},{2,34},{34,66},{66,9... | collective-permute-start | bytes 491528 | tf_op jit(solution)/shard_map/ppermute | solution.py:24
  556.9 8.0 %collective-permute-start.37 = (f32[5,1,32,256]{3,2,1,0:T(8,128)S(1)}, f32[5,1,32,256]{3,2,1,0:T(8,128)S(1)}, u32[]{:S(2)}, u32[]{:S(2)}) collective-permute-start(f32[5,1,32,256]{3,2,1,0:T(8,128)S(1)} %get-tuple-element.43), channel_id=1, source_target_pairs={{32,0},{64,32},{96,64},{33,1},{65,33},{97,65},{34,2},{66,34},{98,6... | collective-permute-start | bytes 491528 | tf_op jit(solution)/shard_map/ppermute | solution.py:27
  565.2 6.6 %collective-permute-start.38 = (f32[5,34,1,256]{3,2,1,0:T(1,128)S(1)}, f32[5,34,1,256]{3,2,1,0:T(1,128)S(1)}, u32[]{:S(2)}, u32[]{:S(2)}) collective-permute-start(f32[5,34,1,256]{3,2,1,0:T(1,128)S(1)} %get-tuple-element.40), channel_id=1, source_target_pairs={{0,8},{8,16},{16,24},{1,9},{9,17},{17,25},{2,10},{10,18},{18,26},{... | collective-permute-start | bytes 522248 | tf_op jit(solution)/shard_map/ppermute | solution.py:24
  568.5 7.1 %collective-permute-start.39 = (f32[5,34,1,256]{3,2,1,0:T(1,128)S(1)}, f32[5,34,1,256]{3,2,1,0:T(1,128)S(1)}, u32[]{:S(2)}, u32[]{:S(2)}) collective-permute-start(f32[5,34,1,256]{3,2,1,0:T(1,128)S(1)} %get-tuple-element.41), channel_id=1, source_target_pairs={{8,0},{16,8},{24,16},{9,1},{17,9},{25,17},{10,2},{18,10},{26,18},{... | collective-permute-start | bytes 522248 | tf_op jit(solution)/shard_map/ppermute | solution.py:27
  584.5 9.2 %collective-permute-start.41 = (f32[5,34,34,1]{2,3,1,0:T(1,128)}, f32[5,34,34,1]{2,3,1,0:T(1,128)}, u32[]{:S(2)}, u32[]{:S(2)}) collective-permute-start(f32[5,34,34,1]{2,3,1,0:T(1,128)} %copy.107), channel_id=1, source_target_pairs={{1,0},{2,1},{3,2},{4,3},{5,4},{6,5},{7,6},{9,8},{10,9},{11,10},{12... | collective-permute-start | bytes 69368 | tf_op jit(solution)/shard_map/ppermute | solution.py:27
  591.6 5.6 collective-permute-start.40
  (35 other events, 444.4 us)
where the time goes:
time: 647 us; the launch traced here: 638 us
  blocking collectives  192 us (30%)
  other arithmetic  178 us (28%)
  starting transfers between devices  118 us (18%)
  local copies, waits for them, and re-layouts  98.8 us (15%)
  waiting for transfers between devices  49.5 us (8%)
    psum x2, blocking collectives, squares(): return lax.psum(inner(residual, residual), ('bx', 'by', 'bz'))  128 us
    ppermute x18, starting transfers between devices, padded(): lax.ppermute(lax.slice_in_dim(block, block.shape[dim] - width, None, axis...  64.5 us
    psum x1, blocking collectives, on_device(): alpha = norm_now / lax.psum(inner(direction, image), ('bx', 'by', 'bz'))  63.9 us
    ppermute x18, starting transfers between devices, padded(): lax.ppermute(lax.slice_in_dim(block, 0, width, axis=dim), axis, backward)  36.5 us
    reduce_sum x3, other arithmetic, inner(): return jnp.sum(first * second, axis=(1, 2, 3), keepdims=True)  34.7 us
    slice x19, local copies, waits for them, and re-layouts, padded(): lax.slice_in_dim(block, block.shape[dim] - width, None, axis=dim)  30.9 us
    ppermute x18, waiting for transfers between devices, padded(): lax.ppermute(lax.slice_in_dim(block, 0, width, axis=dim), axis, backward)  30.7 us
    add x2, other arithmetic, one_sweep(): return relaxed + RELAX_RATE * free * (neighbours(extended) / 6.0 - relaxed)  28.6 us
  transfers between devices with their start and end apart: 42, of which 22 were waited for; matrix products, arithmetic and copies ran while one was open for 11% of the time, Pallas kernels for 0%

commit v1 on v0

--- a/solution.py
+++ b/solution.py
@@ -161,7 +161,9 @@
     norm_now = squares(residual)
     for step_index in range(CG_ITERS):
         image = mass_apply(direction, masses)
-        alpha = norm_now / lax.psum(inner(direction, image), ("bx", "by", "bz"))
+        alpha = norm_now / jnp.sum(
+            lax.all_gather(inner(direction, image), ("bx", "by", "bz")), axis=0
+        )
         solution = solution + alpha * direction
         residual = residual - alpha * image
         norm_next = squares(residual)

time: 647 us -> 655 us (1.012)
    psum x1 -> x0, blocking collectives: 63.9 us -> none  [on_device(): alpha = norm_now / lax.psum(inner(direction, image), ('bx', 'by', 'bz'))]
    unnamed x0 -> x1, blocking collectives: none -> 63.8 us
where the time goes in v1:
time: 655 us; the launch traced here: 646 us
  blocking collectives  191 us (29%)
  other arithmetic  180 us (27%)
  starting transfers between devices  120 us (18%)
  local copies, waits for them, and re-layouts  105 us (16%)
  waiting for transfers between devices  48 us (7%)
    psum x2, blocking collectives, squares(): return lax.psum(inner(residual, residual), ('bx', 'by', 'bz'))  128 us
    ppermute x18, starting transfers between devices, padded(): lax.ppermute(lax.slice_in_dim(block, block.shape[dim] - width, None, axis...  65.8 us
    unnamed x1, blocking collectives  63.8 us
    ppermute x18, starting transfers between devices, padded(): lax.ppermute(lax.slice_in_dim(block, 0, width, axis=dim), axis, backward)  36.4 us
    reduce_sum x3, other arithmetic, inner(): return jnp.sum(first * second, axis=(1, 2, 3), keepdims=True)  34.8 us
    slice x19, local copies, waits for them, and re-layouts, padded(): lax.slice_in_dim(block, block.shape[dim] - width, None, axis=dim)  31 us
    ppermute x18, waiting for transfers between devices, padded(): lax.ppermute(lax.slice_in_dim(block, 0, width, axis=dim), axis, backward)  29.2 us
    add x2, other arithmetic, one_sweep(): return relaxed + RELAX_RATE * free * (neighbours(extended) / 6.0 - relaxed)  29.1 us
  transfers between devices with their start and end apart: 42, of which 22 were waited for; matrix products, arithmetic and copies ran while one was open for 11% of the time, Pallas kernels for 0%

profile of v1, /device:TPU:1, one launch (start us, length us, event | category | flops | bytes accessed | tf_op | source)
XLA Modules:
  0.0 645.9 jit_solution(1025885558856544190)
XLA Ops:
  1.6 4.0 collective-permute-start
  14.1 5.8 collective-permute-start.2
  31.9 4.0 collective-permute-start.3
  42.5 4.0 collective-permute-start.5
  65.2 5.9 collective-permute-start.7
  71.1 7.7 %fusion.120 = f32[32,32,256]{2,1,0:T(8,128)} fusion(f32[34,34,258]{2,1,0:T(8,128)} %slice_bitcast_fusion.7), kind=kLoop, calls=%fused_computation.316 | loop fusion | flops 2097152 | bytes 9437184 | tf_op jit(solution)/shard_map/mul | solution.py:72
  84.7 16.1 %multiply_reduce_fusion.1 = (f32[3]{0:T(128)}, f32[3]{0:T(128)}, f32[3,32,32,256]{3,2,1,0:T(8,128)}) fusion(f32[1,32,32,256]{3,2,1,0:T(8,128)} %copy-done.4, f32[1,32,32,256]{3,2,1,0:T(8,128)S(1)} %multiply_bitcast_fusion.1, f32[1,32,32,256]{3,2,1,0:T(8,128)S(1)} %get-tuple-element.82, f32[3,34,34,1]{3,2,1,0:T(8,128)} %copy.67, ...), kind=kLoop, calls=%fused_computation.195 | loop fusion | flops 36175864 | bytes 7773304 | tf_op jit(solution)/shard_map/reduce_sum | solution.py:117
  101.5 64.7 %all-reduce.4 = (f32[3,1,1,1]{0,3,2,1:T(1,128)S(1)}, f32[384]{0:T(512)S(1)}) all-reduce(f32[3,1,1,1]{0,3,2,1:T(1,128)} %bitcast.63, f32[384]{0:T(512)S(1)} %dynamic-update-slice), channel_id=1, replica_groups=mesh['bx'=4,'by'=4,'bz'=8] {'bx','by','bz'}, use_global_device_ids=true, to_apply=%region_1.2 | all-reduce | flops 387 | bytes 3096 | tf_op jit(solution)/shard_map/psum | solution.py:146
  169.4 62.9 %psum.15 = f32[3,1,1,1]{0,3,2,1:T(1,128)S(1)} all-reduce(f32[3,1,1,1]{0,3,2,1:T(1,128)S(1)} %bitcast.64), channel_id=1, replica_groups=mesh['bx'=4,'by'=4,'bz'=8] {'bx','by','bz'}, use_global_device_ids=true, to_apply=%region_5.6 | all-reduce | flops 3 | bytes 24 | tf_op jit(solution)/shard_map/psum | solution.py:146
  256.9 5.8 collective-permute-start.13
  274.4 15.9 %fusion.67 = f32[3]{0:T(128)} fusion(f32[3,32,32,256]{3,2,1,0:T(8,128)} %copy-done.6, f32[3,34,34,1]{3,2,1,0:T(8,128)} %copy.71, f32[3,34,1,256]{3,2,1,0:T(1,128)S(1)} %collective-permute-done.12, f32[3,34,1,256]{3,2,1,0:T(1,128)S(1)} %collective-permute-done.11, f32[3,1,32,256]{3,2,1,0:T(8,128)S(1)} %collective-permute-done.10, ...), kind=kLoop, calls=%fused_computation.147 | loop fusion | flops 23592956 | bytes 4627564 | tf_op jit(solution)/shard_map/reduce_sum | solution.py:117
  291.1 63.8 %all-reduce.3 = f32[384]{0:T(512)S(1)} all-reduce(f32[384]{0:T(512)S(1)} %dynamic-update-slice.1), channel_id=3, replica_groups=mesh['bx'=4,'by'=4,'bz'=8] {'bx','by','bz'}, use_global_device_ids=true, to_apply=%add.3 | all-reduce | flops 384 | bytes 3072
  355.8 6.8 %multiply_add_fusion = (f32[3,32,32,256]{3,2,1,0:T(8,128)S(1)}, f32[3,32,32,256]{3,2,1,0:T(8,128)}, f32[3,32,32,256]{3,2,1,0:T(8,128)}) fusion(f32[3,32,32,256]{3,2,1,0:T(8,128)} %param.5, f32[3,32,32,256]{3,2,1,0:T(8,128)} %param.6, f32[3]{0:T(128)S(1)} %fusion.122, f32[1,32,32,256]{3,2,1,0:T(8,128)} %copy-done.4, ...), kind=kLoop, calls=%fused_computation.189 | loop fusion | flops 10223616 | bytes 22020132 | tf_op jit(solution)/shard_map/add | solution.py:177
  371.8 4.0 collective-permute-start.17
  385.1 5.4 collective-permute-start.20
  398.4 14.2 %fusion.57 = f32[3,32,32,256]{3,2,1,0:T(8,128)S(1)} fusion(f32[3,32,32,256]{3,2,1,0:T(8,128)} %copy-done.3, f32[3,34,34,1]{3,2,1,0:T(8,128)} %copy.81, f32[3,34,1,256]{3,2,1,0:T(1,128)S(1)} %copy.75, f32[3,34,1,256]{3,2,1,0:T(1,128)S(1)} %copy.73, f32[3,1,32,256]{3,2,1,0:T(8,128)S(1)} %collective-permute-done.16, ...), kind=kLoop, calls=%fused_computation.119 | loop fusion | flops 21233664 | bytes 7773280 | tf_op jit(solution)/shard_map/add | solution.py:151
  422.2 4.7 collective-permute-start.23
  428.3 4.3 collective-permute-done.34
  441.4 5.6 collective-permute-start.26
  447.0 3.8 collective-permute-start.25
  468.3 14.8 %fusion.48 = f32[3,32,32,256]{3,2,1,0:T(8,128)S(1)} fusion(f32[3,32,32,256]{3,2,1,0:T(8,128)} %copy-done.7, f32[3,34,34,1]{3,2,1,0:T(8,128)} %copy.91, f32[3,34,1,256]{3,2,1,0:T(1,128)S(1)} %copy.85, f32[3,34,1,256]{3,2,1,0:T(1,128)S(1)} %copy.83, f32[3,1,32,256]{3,2,1,0:T(8,128)S(1)} %collective-permute-done.22, ...), kind=kLoop, calls=%fused_computation.92 | loop fusion | flops 21233664 | bytes 7773280 | tf_op jit(solution)/shard_map/add | solution.py:151
  487.9 4.7 select_maximum_fusion
  494.1 4.7 collective-permute-start.29
  513.0 3.9 collective-permute-start.31
  517.0 20.2 %fusion.119 = f32[1,32,32,256]{3,2,1,0:T(8,128)} fusion(f32[32,32,256]{2,1,0:T(8,128)S(1)} %copy-done, f32[32,32,256]{2,1,0:T(8,128)} %param.8, f32[34,34,258]{2,1,0:T(8,128)} %get-tuple-element.39, f32[34,34,258]{2,1,0:T(8,128)} %get-tuple-element.38, f32[34,34,258]{2,1,0:T(8,128)S(1)} %get-tuple-element.37), kind=kLoop, calls=%fused_computation.292 | loop fusion | flops 8126464 | bytes 28311552 | tf_op jit(solution)/shard_map/broadcast_in_dim | solution.py:183
  543.2 16.7 %fusion.129 = (f32[3,32,32,256]{3,2,1,0:T(8,128)S(1)}, f32[3,32,32,256]{3,2,1,0:T(8,128)}) fusion(f32[3,32,32,256]{3,2,1,0:T(8,128)} %copy-done.3, f32[3,32,32,256]{3,2,1,0:T(8,128)} %copy-done.8, f32[3,34,34,1]{3,2,1,0:T(8,128)} %copy.101, f32[3,34,1,256]{3,2,1,0:T(1,128)S(1)} %copy.95, f32[3,1,32,256]{3,2,1,0:T(8,128)S(1)} %collective-permute-done.28, ...), kind=kLoop, calls=%fused_computation.367 | loop fusion | flops 22020096 | bytes 14064736 | tf_op jit(solution)/shard_map/sub | solution.py:183
  567.5 4.2 collective-permute-done.37
  578.6 3.8 collective-permute-done.39
  584.0 3.9 fusion.132
  608.4 16.1 %pad_maximum_fusion = f32[5,34,34,258]{3,2,1,0:T(8,128)S(1)} fusion(f32[5,34,34,1]{3,2,1,0:T(8,128)} %copy.109, f32[5,34,1,256]{3,2,1,0:T(1,128)} %copy-done.21, f32[5,1,32,256]{3,2,1,0:T(8,128)S(1)} %collective-permute-done.37, f32[1,32,32,256]{3,2,1,0:T(8,128)} %fusion.119, f32[1,32,32,256]{3,2,1,0:T(8,128)} %bitcast.52, ...), kind=kLoop, calls=%fused_computation | loop fusion | flops 11929920 | bytes 11929920 | tf_op jit(solution)/shard_map/concatenate | solution.py:28
  628.8 6.0 broadcast_compare_fusion.1
  634.9 9.3 %fusion.84 = f32[2,32,32,256]{3,2,1,0:T(8,128)S(1)} fusion(f32[3,32,32,256]{3,2,1,0:T(8,128)S(1)} %get-tuple-element.26, f32[1,32,32,256]{3,2,1,0:T(8,128)S(1)} %bitcast.58, f32[5,34,34,1]{3,2,1,0:T(8,128)S(1)} %copy-done.14, f32[5,34,1,256]{3,2,1,0:T(1,128)S(1)} %copy-done.22, f32[5,34,1,256]{3,2,1,0:T(1,128)S(1)} %copy-done.20, ...), kind=kLoop, calls=%fused_computation.206 | loop fusion | flops 25690112 | bytes 15926432 | tf_op jit(solution)/shard_map/sub | solution.py:112
  (217 shorter events, 226.4 us)
Async XLA Ops:
  14.1 6.8 %collective-permute-start.2 = (f32[2,33,33,1]{2,0,3,1:T(2,128)S(1)}, f32[2,33,33,1]{2,0,3,1:T(2,128)}, u32[]{:S(2)}, u32[]{:S(2)}) collective-permute-start(f32[2,33,33,1]{2,0,3,1:T(2,128)S(1)} %copy.62), channel_id=1, source_target_pairs={{0,1},{1,2},{2,3},{3,4},{4,5},{5,6},{6,7},{8,9},{9,10},{10,11},{11... | collective-permute-start | bytes 26144 | tf_op jit(solution)/shard_map/ppermute | solution.py:16
  31.9 5.6 collective-permute-start.3
  35.9 5.4 collective-permute-start.4
  42.5 8.3 %collective-permute-start.5 = (f32[3,34,1,256]{3,2,1,0:T(1,128)S(1)}, f32[3,34,1,256]{3,2,1,0:T(1,128)S(1)}, u32[]{:S(2)}, u32[]{:S(2)}) collective-permute-start(f32[3,34,1,256]{3,2,1,0:T(1,128)S(1)} %get-tuple-element.62), channel_id=1, source_target_pairs={{0,8},{8,16},{16,24},{1,9},{9,17},{17,25},{2,10},{10,18},{18,26},{... | collective-permute-start | bytes 313352 | tf_op jit(solution)/shard_map/ppermute | solution.py:24
  46.5 6.8 %collective-permute-start.6 = (f32[3,34,1,256]{3,2,1,0:T(1,128)S(1)}, f32[3,34,1,256]{3,2,1,0:T(1,128)S(1)}, u32[]{:S(2)}, u32[]{:S(2)}) collective-permute-start(f32[3,34,1,256]{3,2,1,0:T(1,128)S(1)} %get-tuple-element.63), channel_id=1, source_target_pairs={{8,0},{16,8},{24,16},{9,1},{17,9},{25,17},{10,2},{18,10},{26,18},{... | collective-permute-start | bytes 313352 | tf_op jit(solution)/shard_map/ppermute | solution.py:27
  62.9 18.8 %collective-permute-start.8 = (f32[3,34,34,1]{2,3,1,0:T(1,128)}, f32[3,34,34,1]{2,3,1,0:T(1,128)}, u32[]{:S(2)}, u32[]{:S(2)}) collective-permute-start(f32[3,34,34,1]{2,3,1,0:T(1,128)} %copy.66), channel_id=1, source_target_pairs={{1,0},{2,1},{3,2},{4,3},{5,4},{6,5},{7,6},{9,8},{10,9},{11,10},{12... | collective-permute-start | bytes 41624 | tf_op jit(solution)/shard_map/ppermute | solution.py:27
  65.2 13.6 %collective-permute-start.7 = (f32[3,34,34,1]{2,3,1,0:T(1,128)}, f32[3,34,34,1]{2,3,1,0:T(1,128)}, u32[]{:S(2)}, u32[]{:S(2)}) collective-permute-start(f32[3,34,34,1]{2,3,1,0:T(1,128)} %copy.64), channel_id=1, source_target_pairs={{0,1},{1,2},{2,3},{3,4},{4,5},{5,6},{6,7},{8,9},{9,10},{10,11},{11... | collective-permute-start | bytes 41624 | tf_op jit(solution)/shard_map/ppermute | solution.py:24
  245.1 5.4 collective-permute-start.12
  256.9 10.9 %collective-permute-start.13 = (f32[3,34,34,1]{2,3,1,0:T(1,128)}, f32[3,34,34,1]{2,3,1,0:T(1,128)}, u32[]{:S(2)}, u32[]{:S(2)}) collective-permute-start(f32[3,34,34,1]{2,3,1,0:T(1,128)} %copy.68), channel_id=1, source_target_pairs={{0,1},{1,2},{2,3},{3,4},{4,5},{5,6},{6,7},{8,9},{9,10},{10,11},{11... | collective-permute-start | bytes 41624 | tf_op jit(solution)/shard_map/ppermute | solution.py:24
  265.7 5.7 collective-permute-start.14
  370.5 5.6 collective-permute-start.18
  371.8 5.8 collective-permute-start.17
  385.1 11.1 %collective-permute-start.20 = (f32[3,34,34,1]{2,1,3,0:T(8,128)}, f32[3,34,34,1]{2,1,3,0:T(8,128)S(1)}, u32[]{:S(2)}, u32[]{:S(2)}) collective-permute-start(f32[3,34,34,1]{2,1,3,0:T(8,128)} %copy.80), channel_id=1, source_target_pairs={{1,0},{2,1},{3,2},{4,3},{5,4},{6,5},{7,6},{9,8},{10,9},{11,10},{12... | collective-permute-start | bytes 41624 | tf_op jit(solution)/shard_map/ppermute | solution.py:27
  416.7 10.2 %collective-permute-start.33 = (f32[3,1,32,256]{3,2,1,0:T(8,128)S(1)}, f32[3,1,32,256]{3,2,1,0:T(8,128)S(1)}, u32[]{:S(2)}, u32[]{:S(2)}) collective-permute-start(f32[3,1,32,256]{3,2,1,0:T(8,128)S(1)} %slice.782), channel_id=1, source_target_pairs={{32,0},{64,32},{96,64},{33,1},{65,33},{97,65},{34,2},{66,34},{98,6... | collective-permute-start | bytes 294920 | tf_op jit(solution)/shard_map/ppermute | solution.py:16
  420.9 11.8 %collective-permute-start.24 = (f32[3,34,1,256]{3,1,2,0:T(8,128)S(1)}, f32[3,34,1,256]{3,1,2,0:T(8,128)S(1)}, u32[]{:S(2)}, u32[]{:S(2)}) collective-permute-start(f32[3,34,1,256]{3,1,2,0:T(8,128)S(1)} %copy.84), channel_id=1, source_target_pairs={{8,0},{16,8},{24,16},{9,1},{17,9},{25,17},{10,2},{18,10},{26,18},{... | collective-permute-start | bytes 313352 | tf_op jit(solution)/shard_map/ppermute | solution.py:27
  422.2 10.7 %collective-permute-start.23 = (f32[3,34,1,256]{3,1,2,0:T(8,128)S(1)}, f32[3,34,1,256]{3,1,2,0:T(8,128)S(1)}, u32[]{:S(2)}, u32[]{:S(2)}) collective-permute-start(f32[3,34,1,256]{3,1,2,0:T(8,128)S(1)} %copy.82), channel_id=1, source_target_pairs={{0,8},{8,16},{16,24},{1,9},{9,17},{17,25},{2,10},{10,18},{18,26},{... | collective-permute-start | bytes 313352 | tf_op jit(solution)/shard_map/ppermute | solution.py:24
  427.0 5.6 collective-permute-start.34
  441.4 24.7 %collective-permute-start.26 = (f32[3,34,34,1]{2,1,3,0:T(8,128)S(1)}, f32[3,34,34,1]{2,1,3,0:T(8,128)S(1)}, u32[]{:S(2)}, u32[]{:S(2)}) collective-permute-start(f32[3,34,34,1]{2,1,3,0:T(8,128)S(1)} %copy.90), channel_id=1, source_target_pairs={{1,0},{2,1},{3,2},{4,3},{5,4},{6,5},{7,6},{9,8},{10,9},{11,10},{12... | collective-permute-start | bytes 41624 | tf_op jit(solution)/shard_map/ppermute | solution.py:27
  447.0 16.8 %collective-permute-start.25 = (f32[3,34,34,1]{2,1,3,0:T(8,128)S(1)}, f32[3,34,34,1]{2,1,3,0:T(8,128)S(1)}, u32[]{:S(2)}, u32[]{:S(2)}) collective-permute-start(f32[3,34,34,1]{2,1,3,0:T(8,128)S(1)} %copy.88), channel_id=1, source_target_pairs={{0,1},{1,2},{2,3},{3,4},{4,5},{5,6},{6,7},{8,9},{9,10},{10,11},{11... | collective-permute-start | bytes 41624 | tf_op jit(solution)/shard_map/ppermute | solution.py:24
  456.2 5.5 collective-permute-start.35
  483.2 9.4 %collective-permute-start.27 = (f32[3,1,32,256]{3,2,1,0:T(8,128)S(1)}, f32[3,1,32,256]{3,2,1,0:T(8,128)S(1)}, u32[]{:S(2)}, u32[]{:S(2)}) collective-permute-start(f32[3,1,32,256]{3,2,1,0:T(8,128)S(1)} %get-tuple-element.64), channel_id=1, source_target_pairs={{0,32},{32,64},{64,96},{1,33},{33,65},{65,97},{2,34},{34,66},{66,9... | collective-permute-start | bytes 294920 | tf_op jit(solution)/shard_map/ppermute | solution.py:24
  486.5 6.0 collective-permute-start.28
  492.8 8.4 %collective-permute-start.30 = (f32[3,34,1,256]{3,1,2,0:T(8,128)S(1)}, f32[3,34,1,256]{3,1,2,0:T(8,128)S(1)}, u32[]{:S(2)}, u32[]{:S(2)}) collective-permute-start(f32[3,34,1,256]{3,1,2,0:T(8,128)S(1)} %copy.94), channel_id=1, source_target_pairs={{8,0},{16,8},{24,16},{9,1},{17,9},{25,17},{10,2},{18,10},{26,18},{... | collective-permute-start | bytes 313352 | tf_op jit(solution)/shard_map/ppermute | solution.py:27
  494.1 7.2 %collective-permute-start.29 = (f32[3,34,1,256]{3,1,2,0:T(8,128)S(1)}, f32[3,34,1,256]{3,1,2,0:T(8,128)S(1)}, u32[]{:S(2)}, u32[]{:S(2)}) collective-permute-start(f32[3,34,1,256]{3,1,2,0:T(8,128)S(1)} %copy.92), channel_id=1, source_target_pairs={{0,8},{8,16},{16,24},{1,9},{9,17},{17,25},{2,10},{10,18},{18,26},{... | collective-permute-start | bytes 313352 | tf_op jit(solution)/shard_map/ppermute | solution.py:24
  511.1 29.0 %collective-permute-start.32 = (f32[3,34,34,1]{2,1,3,0:T(8,128)}, f32[3,34,34,1]{2,1,3,0:T(8,128)}, u32[]{:S(2)}, u32[]{:S(2)}) collective-permute-start(f32[3,34,34,1]{2,1,3,0:T(8,128)} %copy.100), channel_id=1, source_target_pairs={{1,0},{2,1},{3,2},{4,3},{5,4},{6,5},{7,6},{9,8},{10,9},{11,10},{12... | collective-permute-start | bytes 41624 | tf_op jit(solution)/shard_map/ppermute | solution.py:27
  513.0 24.1 %collective-permute-start.31 = (f32[3,34,34,1]{2,1,3,0:T(8,128)}, f32[3,34,34,1]{2,1,3,0:T(8,128)}, u32[]{:S(2)}, u32[]{:S(2)}) collective-permute-start(f32[3,34,34,1]{2,1,3,0:T(8,128)} %copy.98), channel_id=1, source_target_pairs={{0,1},{1,2},{2,3},{3,4},{4,5},{5,6},{6,7},{8,9},{9,10},{10,11},{11... | collective-permute-start | bytes 41624 | tf_op jit(solution)/shard_map/ppermute | solution.py:24
  559.9 7.6 %collective-permute-start.36 = (f32[5,1,32,256]{3,2,1,0:T(8,128)S(1)}, f32[5,1,32,256]{3,2,1,0:T(8,128)S(1)}, u32[]{:S(2)}, u32[]{:S(2)}) collective-permute-start(f32[5,1,32,256]{3,2,1,0:T(8,128)S(1)} %get-tuple-element.42), channel_id=1, source_target_pairs={{0,32},{32,64},{64,96},{1,33},{33,65},{65,97},{2,34},{34,66},{66,9... | collective-permute-start | bytes 491528 | tf_op jit(solution)/shard_map/ppermute | solution.py:24
  563.6 8.0 %collective-permute-start.37 = (f32[5,1,32,256]{3,2,1,0:T(8,128)S(1)}, f32[5,1,32,256]{3,2,1,0:T(8,128)S(1)}, u32[]{:S(2)}, u32[]{:S(2)}) collective-permute-start(f32[5,1,32,256]{3,2,1,0:T(8,128)S(1)} %get-tuple-element.43), channel_id=1, source_target_pairs={{32,0},{64,32},{96,64},{33,1},{65,33},{97,65},{34,2},{66,34},{98,6... | collective-permute-start | bytes 491528 | tf_op jit(solution)/shard_map/ppermute | solution.py:27
  571.9 6.8 %collective-permute-start.38 = (f32[5,34,1,256]{3,2,1,0:T(1,128)S(1)}, f32[5,34,1,256]{3,2,1,0:T(1,128)S(1)}, u32[]{:S(2)}, u32[]{:S(2)}) collective-permute-start(f32[5,34,1,256]{3,2,1,0:T(1,128)S(1)} %get-tuple-element.40), channel_id=1, source_target_pairs={{0,8},{8,16},{16,24},{1,9},{9,17},{17,25},{2,10},{10,18},{18,26},{... | collective-permute-start | bytes 522248 | tf_op jit(solution)/shard_map/ppermute | solution.py:24
  575.3 7.2 %collective-permute-start.39 = (f32[5,34,1,256]{3,2,1,0:T(1,128)S(1)}, f32[5,34,1,256]{3,2,1,0:T(1,128)S(1)}, u32[]{:S(2)}, u32[]{:S(2)}) collective-permute-start(f32[5,34,1,256]{3,2,1,0:T(1,128)S(1)} %get-tuple-element.41), channel_id=1, source_target_pairs={{8,0},{16,8},{24,16},{9,1},{17,9},{25,17},{10,2},{18,10},{26,18},{... | collective-permute-start | bytes 522248 | tf_op jit(solution)/shard_map/ppermute | solution.py:27
  591.4 10.2 %collective-permute-start.41 = (f32[5,34,34,1]{2,3,1,0:T(1,128)}, f32[5,34,34,1]{2,3,1,0:T(1,128)}, u32[]{:S(2)}, u32[]{:S(2)}) collective-permute-start(f32[5,34,34,1]{2,3,1,0:T(1,128)} %copy.107), channel_id=1, source_target_pairs={{1,0},{2,1},{3,2},{4,3},{5,4},{6,5},{7,6},{9,8},{10,9},{11,10},{12... | collective-permute-start | bytes 69368 | tf_op jit(solution)/shard_map/ppermute | solution.py:27
  598.3 6.7 %collective-permute-start.40 = (f32[5,34,34,1]{2,3,1,0:T(1,128)}, f32[5,34,34,1]{2,3,1,0:T(1,128)}, u32[]{:S(2)}, u32[]{:S(2)}) collective-permute-start(f32[5,34,34,1]{2,3,1,0:T(1,128)} %copy.106), channel_id=1, source_target_pairs={{0,1},{1,2},{2,3},{3,4},{4,5},{5,6},{6,7},{8,9},{9,10},{10,11},{11... | collective-permute-start | bytes 69368 | tf_op jit(solution)/shard_map/ppermute | solution.py:24
  (37 other events, 443.5 us)
